TPU v7x, 256 devices: a whole 4x4x8 slice. The times are simulated.
256 devices in a mesh: band: 64 (over z, y, core), tile: 4 (over x).
Axes of the slice: x: 4, y: 4, z: 8, core: 2. Of those that a mesh axis runs over, the one named last changes fastest.
Arguments:
- src_field: bfloat16 [4, 32, 1048576], P(None, None, ('band', 'tile')), may hold values from 0.0009994507 to 1
- weights: bfloat16 [65536, 128, 128], P(('band', 'tile')), may hold values from 0 to 0.05625
- block_slab: int32 [65536], P(('band', 'tile')), may hold values from 0 to 127
- block_dest: int32 [65536, 1], P(('band', 'tile')), may hold values from 0 to 255; in each aligned block of 256 rows (0 to 255, 256 to 511, ...) at most 2 rows name the same one
- block_tile: int32 [65536], P(('band', 'tile')), may hold values from 0 to 31
- prior_total: float32 [32, 1048576], P(None, ('band', 'tile')), may hold values from 0.2 to 4
- gamma_shape: float32 [1048576], P(('band', 'tile')), may hold values from 1 to 10
- gamma_scale: float32 [1048576], P(('band', 'tile')), may hold values from 0.05 to 0.6
Outputs:
- season_total: float32 [32, 1048576], P(None, ('band', 'tile'))
- spi_index: float32 [32, 1048576], P(None, ('band', 'tile'))
Inputs may be any that keep to these rules, and one draw needn't show every extreme that they name: `block_dest`: among the 256 blocks of any one device, each destination is named by at most 2 blocks, a bound that some block reaches.
All inputs are finite; a program needn't handle non-finite values.
Results may differ from a plain program's by a relative error of at most 0.00085.
Values may be sent and summed in bfloat16 or wider, within the bound.
A program may use at most 128 MiB of HBM per device.

v0:
```python
import functools

import jax
import jax.numpy as jnp
from jax import lax
from jax.experimental import pallas as pl
from jax.experimental.pallas import tpu as pltpu
from jax.sharding import PartitionSpec as P

MESH = pl.DeviceIdType.MESH
F32, BF16, I32 = jnp.float32, jnp.bfloat16, jnp.int32

PROB_FLOOR = 0.001
CENTRAL_NUMER = (
    -39.69683028665376,
    220.9460984245205,
    -275.9285104469687,
    138.357751867269,
    -30.66479806614716,
    2.506628277459239,
)
CENTRAL_DENOM = (
    -54.47609879822406,
    161.5858368580409,
    -155.6989798598866,
    66.80131188771972,
    -13.28068155288572,
    1.0,
)
TAIL_NUMER = (
    -0.007784894002430293,
    -0.3223964580411365,
    -2.400758277161838,
    -2.549671010429402,
    4.374664141464968,
    2.938163982698783,
)
TAIL_DENOM = (0.007784695709041462, 0.3224671290700398, 2.445134137142996, 3.754408661907416, 1.0)

NZ, NY, NC, NX = 8, 4, 2, 4
PLANE = NY * NC * NX
DAYS, MEM, TILES, SLABS, BLOCKS = 4, 32, 32, 32, 256
SLOTS = 2 * NZ
ALL_SLABS = NX * SLABS
CHUNKS = 8
MC = MEM // CHUNKS
HALF = NZ // 2
FRACTION_TOP = 512.0
EMPTY = ALL_SLABS << 5
LANCZOS_BASE = 0.99999999999980993227684700473478
LANCZOS = (
    676.520368121885098567009190444019,
    -1259.13921672240287047156078755283,
    771.3234287776530788486528258894,
    -176.61502916214059906584551354,
    12.507343278686904814458936853,
    -0.13857109526572011689554707,
    9.984369578019570859563e-6,
    1.50563273514931155834e-7,
)


def horner(coeffs, value):
    total = coeffs[0]
    for coeff in coeffs[1:]:
        total = total * value + coeff
    return total


def log_gamma(shape):
    less = shape - 1.0
    total = LANCZOS_BASE
    for i, coeff in enumerate(LANCZOS):
        total = total + coeff / (less + float(i + 1))
    shifted = less + 7.5
    return 0.9189385332046727 + (less + 0.5) * jnp.log(shifted) - shifted + jnp.log(total)


def drain(ref, sem):
    pltpu.make_async_copy(ref, ref, sem).wait()


def kernel(
    slab_ref, dest_ref, tile_ref, src_hbm, w_hbm, prior_hbm, shape_ref, scale_ref,
    season_hbm, spi_hbm,
    src_ref, prior_ref, season_ref, spi_ref, table_vmem, table, label_ref, lgamma_ref,
    slabs, w_vmem, stage, sendb, recvb, labels, onehot, part, rs_send, rs_recv, series, prior_rows, season_rows, spi_rows,
    w_sem, src_sem, prior_sem, table_sem, out_sem, ag_send, ag_recv, lab_send, lab_recv, p1_send, p1_recv, rs_send_sem, rs_recv_sem,
):
    band = lax.axis_index("band")
    x = lax.axis_index("tile")
    core = band % NC
    y = (band // NC) % NY
    z = band // (NC * NY)
    me = (y * NC + core) * NX + x

    def peer(offset):
        y2 = (y + offset // (NC * NX)) % NY
        c2 = (core + (offset // NX) % NC) % NC
        x2 = (x + offset % NX) % NX
        return (y2 * NC + c2) * NX + x2, ((z * NY + y2) * NC + c2, x2)

    def z_device(z2):
        return ((z2 * NY + y) * NC + core, x)

    up, down = z_device((z + 1) % NZ), z_device((z + NZ - 1) % NZ)

    src_copy = pltpu.make_async_copy(src_hbm, src_ref, src_sem)
    src_copy.start()
    barrier = pltpu.get_barrier_semaphore()

    def greet(offset, carry):
        pl.semaphore_signal(barrier, inc=1, device_id=peer(offset)[1], device_id_type=MESH)
        return carry

    lax.fori_loop(1, PLANE, greet, 0)
    for device in (up, down):
        pl.semaphore_signal(barrier, inc=1, device_id=device, device_id_type=MESH)

    w_copy = pltpu.make_async_copy(w_hbm, w_vmem, w_sem)
    w_copy.start()
    prior_copy = pltpu.make_async_copy(prior_hbm, prior_ref, prior_sem)
    prior_copy.start()

    src_copy.wait()
    for q in range(SLABS):
        cells = src_ref[:, :, q * 128 : (q + 1) * 128].astype(F32)
        slabs[x * SLABS + q] = (cells[0] + cells[1] + cells[2] + cells[3]).astype(BF16)
    slabs[ALL_SLABS] = jnp.zeros((MEM, 128), BF16)

    pl.semaphore_wait(barrier, PLANE + 1)

    own_slabs = slabs.at[pl.ds(x * SLABS, SLABS)]
    for dx in (1, 3, 2):
        pltpu.make_async_remote_copy(
            src_ref=own_slabs, dst_ref=own_slabs, send_sem=ag_send, recv_sem=ag_recv,
            device_id=(band, (x + dx) % NX), device_id_type=MESH,
        ).start()

    wide = (BLOCKS, 128)
    row = lax.broadcasted_iota(I32, wide, 0)
    wanted = (row % NZ) * PLANE + row // NZ
    lane_id = lax.broadcasted_iota(I32, (1, 128), 1)
    low = jnp.full(wide, 1 << 30, I32)
    high = jnp.full(wide, -1, I32)
    for half in range(BLOCKS // 128):
        at = slice(half, half + 1)
        key = (lane_id + 128 * half) * 8192 + slab_ref[at, :] * 32 + tile_ref[at, :]
        named = wanted == dest_ref[at, :]
        low = jnp.minimum(low, jnp.where(named, key, 1 << 30))
        high = jnp.maximum(high, jnp.where(named, key, -1))
    low = jnp.broadcast_to(jnp.min(low, axis=1, keepdims=True), wide)
    high = jnp.broadcast_to(jnp.max(high, axis=1, keepdims=True), wide)
    has_first, has_last = high >= 0, high > low
    first = jnp.where(has_first, low, EMPTY)
    last = jnp.where(has_last, high, EMPTY)
    for half in range(BLOCKS // 128):
        at = slice(half * 128, half * 128 + 128)
        table_vmem[half : half + 1, :] = first[at].T[0:1, :]
        table_vmem[2 + half : 3 + half, :] = last[at].T[0:1, :]
    table_copy = pltpu.make_async_copy(table_vmem, table, table_sem)
    table_copy.start()
    base = (row % NZ) * TILES
    tags = [
        jnp.where(has_first, base + (first & 31), -1).astype(F32).reshape(PLANE, NZ, 128),
        jnp.where(has_last, base + (last & 31), -1).astype(F32).reshape(PLANE, NZ, 128),
    ]
    label_ref[...] = jnp.concatenate(tags, axis=1).astype(BF16)
    labels[me] = label_ref[me]

    def send_labels(offset, carry):
        q2, device = peer(offset)
        pltpu.make_async_remote_copy(
            src_ref=label_ref.at[q2], dst_ref=labels.at[me], send_sem=lab_send, recv_sem=lab_recv,
            device_id=device, device_id_type=MESH,
        ).start()
        return carry

    shape = shape_ref[...]
    lgamma_ref[...] = log_gamma(shape)
    coeff = 1.0 / shape
    series[0] = coeff
    for n in range(1, 65):
        coeff = coeff * (shape + 1.0) / (shape + n)
        series[n] = coeff
    prior_copy.wait()
    for mi in range(MEM // 8):
        for j in range(TILES):
            row = (mi * TILES + j) * 8
            prior_rows[row : row + 8, :] = prior_ref[mi * 8 : mi * 8 + 8, j * 128 : (j + 1) * 128]

    lax.fori_loop(1, PLANE, send_labels, 0)
    table_copy.wait()
    w_copy.wait()
    drain(slabs.at[pl.ds(0, (NX - 1) * SLABS)], ag_recv)

    def pieces(q2):
        for k in range(SLOTS):
            key = table[2 * (k // NZ) + q2 // (128 // NZ), (q2 % (128 // NZ)) * NZ + k % NZ]
            slab = (key >> 5) & 255
            block = key >> 13
            piece = jnp.dot(slabs[slab], w_vmem[block], preferred_element_type=F32)
            stage[pl.ds(k, MEM, stride=SLOTS), :] = piece

    def p1_copy(chunk, offset):
        q2, device = peer(offset)
        return pltpu.make_async_remote_copy(
            src_ref=sendb.at[chunk, q2], dst_ref=recvb.at[chunk, me], send_sem=p1_send.at[chunk],
            recv_sem=p1_recv.at[chunk], device_id=device, device_id_type=MESH,
        )

    rows = MC * SLOTS

    def produce(offset, carry):
        q2, _ = peer(offset)
        pieces(q2)
        for chunk in range(CHUNKS):
            sendb[chunk, q2] = stage[chunk * rows : (chunk + 1) * rows, :].astype(BF16)

        @pl.when(offset > 1)
        def _():
            p1_copy(0, offset - 1).start()

        return carry

    lax.fori_loop(1, PLANE, produce, 0)
    pieces(me)
    for chunk in range(CHUNKS):
        recvb[chunk, me] = stage[chunk * rows : (chunk + 1) * rows, :].astype(BF16)
    p1_copy(0, PLANE - 1).start()

    def send_chunk(step, carry):
        p1_copy(1 + step // (PLANE - 1), 1 + step % (PLANE - 1)).start()
        return carry

    lax.fori_loop(0, (CHUNKS - 1) * (PLANE - 1), send_chunk, 0)

    drain(labels.at[pl.ds(0, PLANE - 1)], lab_recv)
    got = labels[...].astype(F32).reshape(PLANE * SLOTS, 128)
    lane = lax.broadcasted_iota(I32, (PLANE * SLOTS, 128), 1).astype(F32)
    for half in range(NZ * TILES // 128):
        hit = jnp.where(got == lane + 128.0 * half, 1.0, 0.0)
        onehot[half * 128 : (half + 1) * 128, :] = hit.T.astype(BF16)

    def rs_copy(chunk, step, way):
        span = slice(16 * way, 16 * way + 16) if step == 0 else slice(0, TILES)
        return pltpu.make_async_remote_copy(
            src_ref=rs_send.at[way, chunk, step, :, span], dst_ref=rs_recv.at[way, chunk, step, :, span],
            send_sem=rs_send_sem.at[way, chunk, step], recv_sem=rs_recv_sem.at[way, chunk, step],
            device_id=down if way else up, device_id_type=MESH,
        )

    group = 16

    def tail(chunk, g):
        lo = pl.multiple_of(group * g, group)
        cells = pl.ds(lo, group)
        a = shape_ref[cells, :]
        inv_scale = 1.0 / scale_ref[cells, :]
        inv_border = 1.0 / (a + 1.0)

        def member_rows(m):
            member = chunk * MC + m
            return pl.ds((member // 8) * (TILES * 8) + g * (8 * group) + member % 8, group, stride=8)

        remapped = part[chunk, :, pl.ds(pl.multiple_of(z * TILES + group * g, group), group), :]
        remapped = remapped + rs_recv[0, chunk, HALF - 1, :, cells, :].astype(F32)
        remapped = remapped + rs_recv[1, chunk, HALF - 1, :, cells, :].astype(F32)
        season = remapped + jnp.stack([prior_rows[member_rows(m), :] for m in range(MC)])
        for m in range(MC):
            season_rows[member_rows(m), :] = season[m]
        value = season * inv_scale
        border = a + 1.0
        below = value < border
        prefactor = jnp.exp(a * jnp.log(value) - value - lgamma_ref[cells, :])

        ratio = jnp.minimum(value, border) * inv_border
        total = jnp.zeros_like(ratio) + series[64, cells, :]
        for n in range(63, -1, -1):
            total = total * ratio + series[n, cells, :]

        shifted = jnp.clip(value, border, FRACTION_TOP) - a
        quot = 1.0 / (shifted + 129.0)
        for top in range(64, 0, -8):
            older, newer = None, None
            for i in range(top, top - 8, -1):
                step_a = (a - float(i)) * float(i)
                denom = shifted + float(2 * i - 1)
                if newer is None:
                    older, newer = 1.0, denom + step_a * quot
                else:
                    older, newer = newer, denom * newer + step_a * older
            quot = older / newer

        prob = jnp.where(below, total * prefactor, 1.0 - quot * prefactor)
        prob = jnp.clip(prob, PROB_FLOOR, 1.0 - PROB_FLOOR)
        centred = prob - 0.5
        square = centred * centred
        low, high = prob < 0.02425, prob > 0.97575
        root = jnp.sqrt(-2.0 * jnp.log(jnp.where(high, 1.0 - prob, prob)))
        tail_numer = horner(TAIL_NUMER, root)
        numer = jnp.where(low, tail_numer, centred * horner(CENTRAL_NUMER, square))
        numer = jnp.where(high, -tail_numer, numer)
        denom = jnp.where(low | high, horner(TAIL_DENOM, root), horner(CENTRAL_DENOM, square))
        spi = numer / denom
        for m in range(MC):
            spi_rows[member_rows(m), :] = spi[m]

    def gather_sums(chunk):
        drain(recvb.at[chunk, pl.ds(0, PLANE - 1)], p1_recv.at[chunk])
        for m in range(0, MC, 2):
            both = [
                recvb[chunk, :, (m + e) * SLOTS : (m + e + 1) * SLOTS, :].reshape(PLANE * SLOTS, 128)
                for e in range(2)
            ]
            sums = jnp.dot(onehot[...], jnp.concatenate(both, axis=1), preferred_element_type=F32)
            part[chunk, m] = sums[:, :128]
            part[chunk, m + 1] = sums[:, 128:]

    def ring_step(chunk, step):
        hops = HALF - step
        for way in range(2):
            dest = (z + hops) % NZ if way == 0 else (z + NZ - hops) % NZ
            if step == 0:
                at = pl.multiple_of(dest * TILES + 16 * way, 16)
                mine = part[chunk, :, pl.ds(at, 16), :]
                rs_send[way, chunk, 0, :, 16 * way : 16 * way + 16, :] = mine.astype(BF16)
                continue
            rs_copy(chunk, step - 1, way).wait_recv()
            mine = part[chunk, :, pl.ds(pl.multiple_of(dest * TILES, TILES), TILES), :]
            if step == 1:
                other = rs_recv[way, chunk, 0, :, 16 * way : 16 * way + 16, :].astype(F32)
                own_half = mine[:, 16 * way : 16 * way + 16, :] + other
                halves = [own_half, mine[:, 16:, :]] if way == 0 else [mine[:, :16, :], own_half]
                total = jnp.concatenate(halves, axis=1)
            else:
                total = mine + rs_recv[way, chunk, step - 1].astype(F32)
            rs_send[way, chunk, step] = total.astype(BF16)
        for way in range(2):
            rs_copy(chunk, step, way).start()

    def out_copies(mi):
        at = pl.ds(pl.multiple_of(mi * 8, 8), 8)
        return [
            pltpu.make_async_copy(season_ref.at[at], season_hbm.at[at], out_sem.at[0, mi]),
            pltpu.make_async_copy(spi_ref.at[at], spi_hbm.at[at], out_sem.at[1, mi]),
        ]

    def finish(chunk):
        for way in range(2):
            rs_copy(chunk, HALF - 1, way).wait_recv()

        def tail_group(g, inner):
            tail(chunk, g)
            return inner

        lax.fori_loop(0, TILES // group, tail_group, 0)

        @pl.when((chunk + 1) * MC % 8 == 0)
        def _():
            mi = chunk * MC // 8
            at = pl.ds(pl.multiple_of(mi * 8, 8), 8)
            for j in range(TILES):
                rows = pl.ds(pl.multiple_of((mi * TILES + j) * 8, 8), 8)
                season_ref[at, j * 128 : (j + 1) * 128] = season_rows[rows, :]
                spi_ref[at, j * 128 : (j + 1) * 128] = spi_rows[rows, :]
            for copy in out_copies(mi):
                copy.start()

    def iterate(it, carry):
        @pl.when(it < CHUNKS)
        def _():
            gather_sums(it)
            ring_step(it, 0)

        for step in range(HALF - 1, 0, -1):

            @pl.when((it >= step) & (it < CHUNKS + step))
            def _(step=step):
                ring_step(it - step, step)

        @pl.when(it >= HALF)
        def _():
            finish(it - HALF)

        return carry

    lax.fori_loop(0, CHUNKS + HALF, iterate, 0)

    drain(slabs.at[pl.ds(0, (NX - 1) * SLABS)], ag_send)
    drain(labels.at[pl.ds(0, PLANE - 1)], lab_send)

    def settle(chunk, carry):
        drain(sendb.at[chunk, pl.ds(0, PLANE - 1)], p1_send.at[chunk])
        for step in range(HALF):
            for way in range(2):
                rs_copy(chunk, step, way).wait_send()
        return carry

    lax.fori_loop(0, CHUNKS, settle, 0)
    for mi in range(MEM // 8):
        for copy in out_copies(mi):
            copy.wait()


def shards(src_field, weights, block_slab, block_dest, block_tile, prior_total, gamma_shape, gamma_scale):
    vmem = pl.BlockSpec(memory_space=pltpu.VMEM)
    hbm = pl.BlockSpec(memory_space=pl.ANY)
    dma = pltpu.SemaphoreType.DMA
    cells = (TILES, 128)
    return pl.pallas_call(
        kernel,
        out_shape=[jax.ShapeDtypeStruct(prior_total.shape, F32)] * 2,
        in_specs=[vmem, vmem, vmem, hbm, hbm, hbm, vmem, vmem],
        out_specs=[hbm, hbm],
        scratch_shapes=[
            pltpu.VMEM((DAYS, MEM, SLABS * 128), BF16),
            pltpu.VMEM((MEM, TILES * 128), F32),
            pltpu.VMEM((MEM, TILES * 128), F32),
            pltpu.VMEM((MEM, TILES * 128), F32),
            pltpu.VMEM((4, 128), I32),
            pltpu.SMEM((4, 128), I32),
            pltpu.VMEM((PLANE, SLOTS, 128), BF16),
            pltpu.VMEM((TILES, 128), F32),
            pltpu.VMEM((ALL_SLABS + 1, MEM, 128), BF16),
            pltpu.VMEM((BLOCKS, 128, 128), BF16),
            pltpu.VMEM((MEM * SLOTS, 128), F32),
            pltpu.VMEM((CHUNKS, PLANE, MC * SLOTS, 128), BF16),
            pltpu.VMEM((CHUNKS, PLANE, MC * SLOTS, 128), BF16),
            pltpu.VMEM((PLANE, SLOTS, 128), BF16),
            pltpu.VMEM((NZ * TILES, PLANE * SLOTS), BF16),
            pltpu.VMEM((CHUNKS, MC, NZ * TILES, 128), F32),
            pltpu.VMEM((2, CHUNKS, HALF, MC, TILES, 128), BF16),
            pltpu.VMEM((2, CHUNKS, HALF, MC, TILES, 128), BF16),
            pltpu.VMEM((65, TILES, 128), F32),
            pltpu.VMEM((MEM * TILES, 128), F32),
            pltpu.VMEM((MEM * TILES, 128), F32),
            pltpu.VMEM((MEM * TILES, 128), F32),
            dma, dma, dma, dma, dma((2, MEM // 8)), dma, dma, dma, dma, dma((CHUNKS,)), dma((CHUNKS,)), dma((2, CHUNKS, HALF)), dma((2, CHUNKS, HALF)),
        ],
        compiler_params=pltpu.CompilerParams(
            collective_id=0, has_side_effects=True, vmem_limit_bytes=56 * 1024 * 1024
        ),
        name="remap_spi",
    )(
        block_slab.reshape(BLOCKS // 128, 128),
        block_dest.reshape(BLOCKS // 128, 128),
        block_tile.reshape(BLOCKS // 128, 128),
        src_field,
        weights,
        prior_total,
        gamma_shape.reshape(cells),
        gamma_scale.reshape(cells),
    )


def solution(mesh):
    placed = (
        P(None, None, ("band", "tile")),
        P(("band", "tile"), None, None),
        P(("band", "tile")),
        P(("band", "tile"), None),
        P(("band", "tile")),
        P(None, ("band", "tile")),
        P(("band", "tile")),
        P(("band", "tile")),
    )
    return jax.shard_map(
        lambda *arrays: tuple(shards(*arrays)),
        mesh=mesh,
        in_specs=placed,
        out_specs=(P(None, ("band", "tile")), P(None, ("band", "tile"))),
        check_vma=False,
    )
```

profile of v0, /device:TPU:2, one launch (start us, length us, event | category | flops | bytes accessed | tf_op | source)
XLA Modules:
  0.0 99.9 jit_solution(9631577557897903181)
XLA Ops:
  0.6 95.5 %remap_spi.1 = (f32[32,4096]{1,0:T(8,128)}, f32[32,4096]{1,0:T(8,128)}) custom-call(s32[2,128]{1,0:T(2,128)} %bitcast.7, s32[2,128]{1,0:T(2,128)} %bitcast.8, s32[2,128]{1,0:T(2,128)} %bitcast.9, bf16[4,32,4096]{2,1,0:T(8,128)(2,1)} %src_hbm.1, bf16[256,128,128]{2,1,0:T(8,128)(2,1)} %w_hbm.1, f32[32,4096]{1,0:T(8,128)} %prior_hbm.1, f32[32,128]{1,0:T(8,128)} %bitcast.5, ...), custom_call_target="tpu_custom_call" | custom-call | tf_op jit(solution)/shard_map/remap_spi/pallas_call | solution.py:411
  96.2 1.9 %copy.12 = f32[32,4096]{1,0:T(8,128)} copy(f32[32,4096]{1,0:T(8,128)} %get-tuple-element.4) | data formatting | bytes 1048576
  98.0 1.9 %copy.13 = f32[32,4096]{1,0:T(8,128)} copy(f32[32,4096]{1,0:T(8,128)} %get-tuple-element.5) | data formatting | bytes 1048576
where the time goes:
time: 101 us; the launch traced here: 99.9 us
  Pallas kernels  95.5 us (95%)
  local copies, waits for them, and re-layouts  3.74 us (4%)
    pallas_call x1, Pallas kernels, shards(): pl.pallas_call(kernel, out_shape=[jax.ShapeDtypeStruct(prior_total.shape,...  95.5 us
    unnamed x2, local copies, waits for them, and re-layouts  3.74 us

commit v1 on v0

--- a/solution.py
+++ b/solution.py
@@ -45,6 +45,7 @@
 CHUNKS = 8
 MC = MEM // CHUNKS
 HALF = NZ // 2
+FIRST = 2
 FRACTION_TOP = 512.0
 EMPTY = ALL_SLABS << 5
 LANCZOS_BASE = 0.99999999999980993227684700473478
@@ -81,11 +82,11 @@
 
 
 def kernel(
-    slab_ref, dest_ref, tile_ref, src_hbm, w_hbm, prior_hbm, shape_ref, scale_ref,
+    slab_hbm, dest_hbm, tile_hbm, src_hbm, w_hbm, prior_hbm, shape_hbm, scale_hbm,
     season_hbm, spi_hbm,
-    src_ref, prior_ref, season_ref, spi_ref, table_vmem, table, label_ref, lgamma_ref,
+    slab_ref, dest_ref, tile_ref, shape_ref, scale_ref, src_ref, prior_ref, season_ref, spi_ref, table_vmem, table, label_ref, lgamma_ref,
     slabs, w_vmem, stage, sendb, recvb, labels, onehot, part, rs_send, rs_recv, series, prior_rows, season_rows, spi_rows,
-    w_sem, src_sem, prior_sem, table_sem, out_sem, ag_send, ag_recv, lab_send, lab_recv, p1_send, p1_recv, rs_send_sem, rs_recv_sem,
+    small_sem, w_sem, src_sem, prior_sem, table_sem, out_sem, ag_send, ag_recv, lab_send, lab_recv, p1_send, p1_recv, rs_send_sem, rs_recv_sem,
 ):
     band = lax.axis_index("band")
     x = lax.axis_index("tile")
@@ -95,9 +96,9 @@
     me = (y * NC + core) * NX + x
 
     def peer(offset):
-        y2 = (y + offset // (NC * NX)) % NY
-        c2 = (core + (offset // NX) % NC) % NC
-        x2 = (x + offset % NX) % NX
+        y2 = lax.rem(y + offset + lax.div(offset, NX), NY)
+        c2 = lax.rem(core + lax.div(offset, NX * NY), NC)
+        x2 = lax.rem(x + offset, NX)
         return (y2 * NC + c2) * NX + x2, ((z * NY + y2) * NC + c2, x2)
 
     def z_device(z2):
@@ -121,6 +122,14 @@
     w_copy.start()
     prior_copy = pltpu.make_async_copy(prior_hbm, prior_ref, prior_sem)
     prior_copy.start()
+    small_copies = [
+        pltpu.make_async_copy(there, here, small_sem.at[i])
+        for i, (there, here) in enumerate(
+            [(slab_hbm, slab_ref), (dest_hbm, dest_ref), (tile_hbm, tile_ref), (shape_hbm, shape_ref), (scale_hbm, scale_ref)]
+        )
+    ]
+    for copy in small_copies:
+        copy.start()
 
     src_copy.wait()
     for q in range(SLABS):
@@ -130,13 +139,22 @@
 
     pl.semaphore_wait(barrier, PLANE + 1)
 
-    own_slabs = slabs.at[pl.ds(x * SLABS, SLABS)]
-    for dx in (1, 3, 2):
-        pltpu.make_async_remote_copy(
-            src_ref=own_slabs, dst_ref=own_slabs, send_sem=ag_send, recv_sem=ag_recv,
-            device_id=(band, (x + dx) % NX), device_id_type=MESH,
-        ).start()
-
+    half_slabs = SLABS // 2
+
+    def ag_copy(owner, half, way, sem):
+        at = slabs.at[pl.ds(owner * SLABS + half * half_slabs, half_slabs)]
+        x2 = (x + NX - 1) % NX if way else (x + 1) % NX
+        return pltpu.make_async_remote_copy(
+            src_ref=at, dst_ref=at, send_sem=ag_send.at[sem], recv_sem=ag_recv.at[sem],
+            device_id=(band, x2), device_id_type=MESH,
+        )
+
+    own_copies = [ag_copy(x, way if turn == 0 else 1 - way, way, 2 * way + turn) for turn in range(2) for way in range(2)]
+    for copy in own_copies:
+        copy.start()
+
+    for copy in small_copies:
+        copy.wait()
     wide = (BLOCKS, 128)
     row = lax.broadcasted_iota(I32, wide, 0)
     wanted = (row % NZ) * PLANE + row // NZ
@@ -189,10 +207,17 @@
             row = (mi * TILES + j) * 8
             prior_rows[row : row + 8, :] = prior_ref[mi * 8 : mi * 8 + 8, j * 128 : (j + 1) * 128]
 
+    passed_on = []
+    for way in range(2):
+        own_copies[way].wait_recv()
+        owner = (x + 1) % NX if way else (x + NX - 1) % NX
+        passed_on.append(ag_copy(owner, way, way, 4 + way))
+        passed_on[way].start()
     lax.fori_loop(1, PLANE, send_labels, 0)
     table_copy.wait()
     w_copy.wait()
-    drain(slabs.at[pl.ds(0, (NX - 1) * SLABS)], ag_recv)
+    for copy in own_copies[2:] + passed_on:
+        copy.wait_recv()
 
     def pieces(q2):
         for k in range(SLOTS):
@@ -219,7 +244,8 @@
 
         @pl.when(offset > 1)
         def _():
-            p1_copy(0, offset - 1).start()
+            for chunk in range(FIRST):
+                p1_copy(chunk, offset - 1).start()
 
         return carry
 
@@ -227,13 +253,17 @@
     pieces(me)
     for chunk in range(CHUNKS):
         recvb[chunk, me] = stage[chunk * rows : (chunk + 1) * rows, :].astype(BF16)
-    p1_copy(0, PLANE - 1).start()
-
-    def send_chunk(step, carry):
-        p1_copy(1 + step // (PLANE - 1), 1 + step % (PLANE - 1)).start()
-        return carry
-
-    lax.fori_loop(0, (CHUNKS - 1) * (PLANE - 1), send_chunk, 0)
+    for chunk in range(FIRST):
+        p1_copy(chunk, PLANE - 1).start()
+
+    def send_chunk(chunk):
+        def send(offset, carry):
+            p1_copy(chunk, offset).start()
+            return carry
+
+        lax.fori_loop(1, PLANE, send, 0)
+
+    send_chunk(FIRST)
 
     drain(labels.at[pl.ds(0, PLANE - 1)], lab_recv)
     got = labels[...].astype(F32).reshape(PLANE * SLOTS, 128)
@@ -368,12 +398,16 @@
                 copy.start()
 
     def iterate(it, carry):
+        @pl.when(it < CHUNKS - FIRST - 1)
+        def _():
+            send_chunk(it + FIRST + 1)
+
         @pl.when(it < CHUNKS)
         def _():
             gather_sums(it)
             ring_step(it, 0)
 
-        for step in range(HALF - 1, 0, -1):
+        for step in range(1, HALF):
 
             @pl.when((it >= step) & (it < CHUNKS + step))
             def _(step=step):
@@ -387,7 +421,8 @@
 
     lax.fori_loop(0, CHUNKS + HALF, iterate, 0)
 
-    drain(slabs.at[pl.ds(0, (NX - 1) * SLABS)], ag_send)
+    for copy in own_copies + passed_on:
+        copy.wait_send()
     drain(labels.at[pl.ds(0, PLANE - 1)], lab_send)
 
     def settle(chunk, carry):
@@ -404,16 +439,19 @@
 
 
 def shards(src_field, weights, block_slab, block_dest, block_tile, prior_total, gamma_shape, gamma_scale):
-    vmem = pl.BlockSpec(memory_space=pltpu.VMEM)
-    hbm = pl.BlockSpec(memory_space=pl.ANY)
     dma = pltpu.SemaphoreType.DMA
     cells = (TILES, 128)
     return pl.pallas_call(
         kernel,
         out_shape=[jax.ShapeDtypeStruct(prior_total.shape, F32)] * 2,
-        in_specs=[vmem, vmem, vmem, hbm, hbm, hbm, vmem, vmem],
-        out_specs=[hbm, hbm],
+        in_specs=[pl.BlockSpec(memory_space=pl.ANY)] * 8,
+        out_specs=[pl.BlockSpec(memory_space=pl.ANY)] * 2,
         scratch_shapes=[
+            pltpu.VMEM((BLOCKS // 128, 128), I32),
+            pltpu.VMEM((BLOCKS // 128, 128), I32),
+            pltpu.VMEM((BLOCKS // 128, 128), I32),
+            pltpu.VMEM(cells, F32),
+            pltpu.VMEM(cells, F32),
             pltpu.VMEM((DAYS, MEM, SLABS * 128), BF16),
             pltpu.VMEM((MEM, TILES * 128), F32),
             pltpu.VMEM((MEM, TILES * 128), F32),
@@ -436,22 +474,25 @@
             pltpu.VMEM((MEM * TILES, 128), F32),
             pltpu.VMEM((MEM * TILES, 128), F32),
             pltpu.VMEM((MEM * TILES, 128), F32),
-            dma, dma, dma, dma, dma((2, MEM // 8)), dma, dma, dma, dma, dma((CHUNKS,)), dma((CHUNKS,)), dma((2, CHUNKS, HALF)), dma((2, CHUNKS, HALF)),
+            dma((5,)), dma, dma, dma, dma, dma((2, MEM // 8)), dma((6,)), dma((6,)), dma, dma, dma((CHUNKS,)), dma((CHUNKS,)), dma((2, CHUNKS, HALF)), dma((2, CHUNKS, HALF)),
         ],
         compiler_params=pltpu.CompilerParams(
-            collective_id=0, has_side_effects=True, vmem_limit_bytes=56 * 1024 * 1024
+            collective_id=0, has_side_effects=True, vmem_limit_bytes=34 * 1024 * 1024
         ),
         name="remap_spi",
-    )(
-        block_slab.reshape(BLOCKS // 128, 128),
-        block_dest.reshape(BLOCKS // 128, 128),
-        block_tile.reshape(BLOCKS // 128, 128),
-        src_field,
-        weights,
-        prior_total,
-        gamma_shape.reshape(cells),
-        gamma_scale.reshape(cells),
-    )
+    )(*[
+        pltpu.with_memory_space_constraint(array, pltpu.HBM)
+        for array in (
+            block_slab.reshape(BLOCKS // 128, 128),
+            block_dest.reshape(BLOCKS // 128, 128),
+            block_tile.reshape(BLOCKS // 128, 128),
+            src_field,
+            weights,
+            prior_total,
+            gamma_shape.reshape(cells),
+            gamma_scale.reshape(cells),
+        )
+    ])
 
 
 def solution(mesh):

time: 101 us -> 89.2 us (0.88); the launches traced: 99.9 us -> 89.1 us
  Pallas kernels: 95.5 us -> 86.9 us
  local copies, waits for them, and re-layouts: 3.74 us -> 1.59 us
    pallas_call x1, Pallas kernels: 95.5 us -> 86.9 us  [shards(): pl.pallas_call(kernel, out_shape=[jax.ShapeDtypeStruct(prior_total.shape,...]
    unnamed x2, local copies, waits for them, and re-layouts: 3.74 us -> 1.59 us
where the time goes in v1:
time: 89.2 us; the launch traced here: 89.1 us
  Pallas kernels  86.9 us (97%)
  local copies, waits for them, and re-layouts  1.59 us (2%)
    pallas_call x1, Pallas kernels, shards(): pl.pallas_call(kernel, out_shape=[jax.ShapeDtypeStruct(prior_total.shape,...  86.9 us

profile of v1, /device:TPU:2, one launch (start us, length us, event | category | flops | bytes accessed | tf_op | source)
XLA Modules:
  0.0 89.1 jit_solution(6101488603352692981)
XLA Ops:
  0.6 86.9 %remap_spi.1 = (f32[32,4096]{1,0:T(8,128)S(1)}, f32[32,4096]{1,0:T(8,128)S(1)}) custom-call(s32[2,128]{1,0:T(2,128)} %bitcast.7, s32[2,128]{1,0:T(2,128)} %bitcast.8, s32[2,128]{1,0:T(2,128)} %bitcast.9, bf16[4,32,4096]{2,1,0:T(8,128)(2,1)} %src_hbm.1, bf16[256,128,128]{2,1,0:T(8,128)(2,1)} %w_hbm.1, f32[32,4096]{1,0:T(8,128)} %prior_hbm.1, ...), custom_call_target="tpu_custom_call" | custom-call | tf_op jit(solution)/shard_map/remap_spi/pallas_call | solution.py:444
  87.6 0.8 copy.12
  88.3 0.8 copy.13
